TPU v7x, 32 devices: a whole 2x2x4 slice. The times are simulated.
32 devices in a mesh: row: 4 (over x, core), col: 8 (over z, y).
Axes of the slice: x: 2, y: 2, z: 4, core: 2. Of those that a mesh axis runs over, the one named last changes fastest.
Arguments:
- centres: float32 [65536, 64], P(('row', 'col')), may hold values from -6 to 6
- weights: float32 [65536, 64], P(('row', 'col')), may hold values from -0.25 to 0.25
- targets: float32 [512, 64], replicated, may hold values from -6 to 6
- batch_index: int32 [512], replicated, may hold values from 0 to 65535
- nystrom_index: int32 [4096], replicated, may hold values from 0 to 65535
- eigvecs: float32 [4096, 1024], P('row', 'col'), may hold values from -0.09375 to 0.09375
- mode_scale: float32 [1024], P('col'), may hold values from 0.02 to 0.2
Outputs:
- residual: float32 [512, 64], replicated
- step: float32 [65536, 64], P(('row', 'col'))
All inputs are finite; a program needn't handle non-finite values.
Results may differ from a plain program's by a relative error of at most 0.0001.
Values sent between devices are 32-bit elements; how exact they have to be, the bound alone decides.
A program may use at most 128 MiB of HBM per device.

v0:
```python
import jax
import jax.numpy as jnp
from jax import lax
from jax.sharding import PartitionSpec as P

learning_rate = 0.25


def kernel(left, right):
    left_sq = jnp.sum(left * left, axis=1)
    right_sq = jnp.sum(right * right, axis=1)
    inner_prod = jnp.dot(
        left, right.T, precision=lax.Precision.HIGHEST, preferred_element_type=jnp.float32
    )
    return jnp.exp(
        -(left_sq[:, None] + right_sq[None, :] - 2.0 * inner_prod) / float(left.shape[1])
    )


def product(left, right):
    return jnp.dot(left, right, precision=lax.Precision.HIGHEST, preferred_element_type=jnp.float32)


def local(centres, weights, targets, batch_index, nystrom_index, eigvecs, mode_scale):
    rows_dev = centres.shape[0]
    block_rows = eigvecs.shape[0]
    offset = lax.axis_index(("row", "col")) * rows_dev

    def select_rows(index):
        local_rows = index - offset
        inside = (local_rows >= 0) & (local_rows < rows_dev)
        fetched = jnp.take(centres, jnp.clip(local_rows, 0, rows_dev - 1), axis=0)
        return jnp.where(inside[:, None], fetched, 0.0)

    batch_feats, nystrom = lax.psum(
        (select_rows(batch_index), select_rows(nystrom_index)), ("row", "col")
    )
    nys_block = lax.dynamic_slice_in_dim(nystrom, lax.axis_index("row") * block_rows, block_rows, 0)
    kern_batch = kernel(centres, batch_feats)
    partial_pred = lax.dot_general(
        kern_batch,
        weights,
        (((0,), (0,)), ((), ())),
        precision=lax.Precision.HIGHEST,
        preferred_element_type=jnp.float32,
    )
    prediction = lax.psum(partial_pred, ("row", "col"))
    residual = prediction - targets
    gradient = product(kernel(nys_block, batch_feats), residual)
    mode_terms = lax.dot_general(
        eigvecs,
        gradient,
        (((0,), (0,)), ((), ())),
        precision=lax.Precision.HIGHEST,
        preferred_element_type=jnp.float32,
    )
    coeff = mode_scale[:, None] * lax.psum(mode_terms, "row")
    correction = lax.psum(product(eigvecs, coeff), "col")
    direct = product(kern_batch, residual)
    folded = direct - product(
        kernel(centres, nystrom), lax.all_gather(correction, "row", axis=0, tiled=True)
    )
    step = learning_rate * folded
    return (residual, step)


def solution(mesh):
    in_specs = (
        P(("row", "col"), None),
        P(("row", "col"), None),
        P(),
        P(),
        P(),
        P("row", "col"),
        P("col"),
    )
    out_specs = (P(), P(("row", "col"), None))
    return jax.shard_map(local, mesh=mesh, in_specs=in_specs, out_specs=out_specs, check_vma=False)
```

profile of v0, /device:TPU:0, one launch (start us, length us, event | category | flops | bytes accessed | tf_op | source)
XLA Modules:
  0.0 467.1 jit_solution(167002956576013100)
XLA Ops:
  7.2 0.7 compare_and_fusion.2
  8.0 1.4 copy.9
  9.4 1.0 gather_fusion
  10.4 0.9 select_select_fusion.1
  11.5 14.2 %gather_fusion.1 = f32[4096,64]{1,0:T(8,128)} fusion(f32[2048,64]{1,0:T(8,128)S(1)} %copy.9, s32[4096]{0:T(1024)S(1)} %fusion.30), kind=kCustom, calls=%fused_computation.1 | custom fusion | bytes 2113536 | tf_op jit(solution)/shard_map/jit(_take)/gather | solution.py:32
  25.7 6.0 %select_select_fusion = f32[4096,64]{1,0:T(8,128)} fusion(f32[4096,64]{1,0:T(8,128)} %gather_fusion.1, pred[4096]{0:T(1024)(128)(4,1)S(1)} %get-tuple-element.7, pred[4096]{0:T(1024)(128)(4,1)S(1)} %get-tuple-element.6), kind=kLoop, calls=%fused_computation.27 | loop fusion | flops 524288 | bytes 2105344 | tf_op jit(solution)/shard_map/jit(_where)/select_n | solution.py:33
  31.8 111.6 %all-reduce.5.cloned.1.call-done = f32[512,64]{1,0:T(8,128)} async-done(((f32[512,64]{1,0:T(8,128)}), f32[512,64]{1,0:T(8,128)}) %all-reduce.5.cloned.1.call-update) | async-done | bytes 131088 | tf_op jit(solution)/shard_map/psum | solution.py:35
  143.3 1.1 multiply_reduce_fusion.3
  144.4 5.1 %fusion.13 = f32[2048,512]{0,1:T(8,128)S(1)} fusion(f32[512,64]{1,0:T(8,128)} %all-reduce.5.cloned.1.call-done, f32[2048,64]{0,1:T(8,128)S(1)} %copy-done.3, f32[512]{0:T(512)S(1)} %multiply_reduce_fusion.3, f32[2048]{0:T(1024)S(1)} %multiply_reduce_fusion.2), kind=kOutput, calls=%fused_computation.16 | convolution fusion | flops 810549248 | bytes 4859904 | tf_op jit(solution)/shard_map/dot_general | solution.py:12
  149.5 2.0 copy-done.1
  151.6 4.8 %fusion.36 = f32[512,64]{0,1:T(8,128)} fusion(f32[2048,512]{0,1:T(8,128)S(1)} %fusion.13, f32[2048,64]{0,1:T(8,128)S(1)} %copy-done.5), kind=kOutput, calls=%fused_computation.55 | convolution fusion | flops 805306368 | bytes 4849664 | tf_op jit(solution)/shard_map/dot_general | solution.py:40
  156.7 134.4 %all-reduce.9.cloned.1.call-done = (f32[512,64]{0,1:T(8,128)}, f32[4096,64]{1,0:T(8,128)}) async-done(((f32[512,64]{0,1:T(8,128)}, f32[4096,64]{1,0:T(8,128)}), (f32[512,64]{0,1:T(8,128)}, f32[4096,64]{1,0:T(8,128)})) %all-reduce.9.cloned.1.call-update) | async-done | bytes 1179664 | tf_op jit(solution)/shard_map/psum | solution.py:47
  291.1 0.9 sub.30
  292.0 1.3 multiply_reduce_fusion.1
  293.3 2.8 fusion.26
  296.2 2.1 fusion.15
  298.3 1.0 convolution_bitcast_fusion.1
  299.3 10.7 %psum.38 = f32[128,64]{1,0:T(8,128)S(1)} all-reduce(f32[128,64]{1,0:T(8,128)S(1)} %convolution_bitcast_fusion.1), channel_id=1, replica_groups=mesh['row'=4,'col'=8] {'row'}, use_global_device_ids=true, to_apply=%region_7.8 | all-reduce | flops 8192 | bytes 65536 | tf_op jit(solution)/shard_map/psum | solution.py:57
  310.0 1.5 convolution_bitcast_fusion
  311.8 0.6 multiply_reduce_fusion
  312.4 69.5 %all-reduce.7.cloned.1.call-done = f32[1024,64]{0,1:T(8,128)} async-done(((f32[1024,64]{0,1:T(8,128)}), f32[1024,64]{0,1:T(8,128)}) %all-reduce.7.cloned.1.call-update) | async-done | bytes 262160 | tf_op jit(solution)/shard_map/psum | solution.py:58
  381.9 30.2 %fusion.37 = f32[4096,2048]{0,1:T(8,128)} fusion(f32[4096,64]{1,0:T(8,128)S(1)} %copy-done.2, f32[2048,64]{0,1:T(8,128)S(1)} %copy-done.3), kind=kOutput, calls=%fused_computation.56 | convolution fusion | flops 6442450944 | bytes 35127296 | tf_op jit(solution)/shard_map/dot_general | solution.py:12
  412.1 42.7 %fusion.3 = f32[2048,64]{0,1:T(8,128)S(1)} fusion(f32[4096,64]{0,1:T(8,128)} %all-gather.2.cloned.1.call-done, f32[4096,2048]{0,1:T(8,128)} %fusion.37, f32[4096]{0:T(1024)S(1)} %multiply_reduce_fusion, f32[2048]{0:T(1024)S(1)} %multiply_reduce_fusion.2), kind=kOutput, calls=%fused_computation.6 | convolution fusion | flops 6484393984 | bytes 35151872 | tf_op jit(solution)/shard_map/dot_general | solution.py:21
  454.8 5.8 %fusion.14 = f32[2048,64]{0,1:T(8,128)} fusion(f32[2048,64]{0,1:T(8,128)S(1)} %fusion.3, f32[2048,512]{0,1:T(8,128)} %copy-done.1, f32[512,64]{0,1:T(8,128)S(1)} %sub.30), kind=kOutput, calls=%fused_computation.18 | convolution fusion | flops 805568512 | bytes 5373952 | tf_op jit(solution)/shard_map/dot_general | solution.py:21
  (32 shorter events, 0.8 us)
Async XLA Ops:
  7.2 291.1 %copy-start = (f32[1024,128]{1,0:T(8,128)S(1)}, f32[1024,128]{1,0:T(8,128)}, u32[]{:S(2)}) copy-start(f32[1024,128]{1,0:T(8,128)} %param.12) | copy-start | bytes 1572868
  7.2 136.2 %all-reduce.5.cloned.1.call-start = ((), (), s32[]{:S(2)}) async-start(), calls=%async_computation | async-start | bytes 524288 | tf_op jit(solution)/shard_map/psum | solution.py:35
  8.0 3.4 copy-start.8
  11.4 279.7 %all-reduce.9.cloned.1.call-start = ((), (), s32[]{:S(2)}) async-start(), calls=%async_computation.3 | async-start | bytes 4456448 | tf_op jit(solution)/shard_map/psum | solution.py:47
  25.7 6.0 %copy-start.3 = (f32[2048,64]{0,1:T(8,128)S(1)}, f32[2048,64]{0,1:T(8,128)}, u32[]{:S(2)}) copy-start(f32[2048,64]{0,1:T(8,128)} %param.7) | copy-start | bytes 1572868
  144.4 7.1 %copy-start.5 = (f32[2048,64]{0,1:T(8,128)S(1)}, f32[2048,64]{0,1:T(8,128)}, u32[]{:S(2)}) copy-start(f32[2048,64]{0,1:T(8,128)} %param.8) | copy-start | bytes 1572868
  149.5 2.0 copy-start.1
  156.4 134.7 %copy-start.7 = (f32[512,64]{0,1:T(8,128)S(1)}, f32[512,64]{0,1:T(8,128)}, u32[]{:S(2)}) copy-start(f32[512,64]{0,1:T(8,128)} %param.9) | copy-start | bytes 393220
  156.4 136.9 %copy-start.4 = (f32[512,64]{1,0:T(8,128)S(1)}, f32[512,64]{1,0:T(8,128)}, u32[]{:S(2)}) copy-start(f32[512,64]{1,0:T(8,128)} %all-reduce.5.cloned.1.call-done) | copy-start | bytes 393220
  156.4 225.5 %all-reduce.7.cloned.1.call-start = ((), (), s32[]{:S(2)}) async-start(), calls=%async_computation.1 | async-start | bytes 524288 | tf_op jit(solution)/shard_map/psum | solution.py:58
  292.0 162.8 %copy-start.6 = (f32[512,64]{0,1:T(8,128)}, f32[512,64]{0,1:T(8,128)S(1)}, u32[]{:S(2)}) copy-start(f32[512,64]{0,1:T(8,128)S(1)} %sub.30) | copy-start | bytes 393220
  296.2 13.8 %copy-start.9 = (f32[128]{0:T(128)S(1)}, f32[128]{0:T(128)}, u32[]{:S(2)}) copy-start(f32[128]{0:T(128)} %param.13) | copy-start | bytes 1540
  296.2 15.5 %copy-start.2 = (f32[4096,64]{1,0:T(8,128)S(1)}, f32[4096,64]{1,0:T(8,128)}, u32[]{:S(2)}) copy-start(f32[4096,64]{1,0:T(8,128)} %get-tuple-element.3) | copy-start | bytes 3145732
  311.5 100.6 %all-gather.2.cloned.1.call-start = ((), (), s32[]{:S(2)}) async-start(), calls=%async_computation.2 | async-start | bytes 1310720 | tf_op jit(solution)/shard_map/all_gather | solution.py:61
Sparse Core Ops, SparseCore 0:
  14.1 129.2 all-reduce.4
  156.6 134.4 all-reduce.8
  311.6 70.2 all-reduce.6
  383.3 15.8 all-gather.1
where the time goes:
time: 468 us; the launch traced here: 467 us
  waiting for transfers between devices  316 us (68%)
  matrix products  95.9 us (20%)
  local copies, waits for them, and re-layouts  18.7 us (4%)
  between operations  14 us (3%)
  other arithmetic  11.7 us (2%)
  blocking collectives  10.7 us (2%)
    psum x1, waiting for transfers between devices, local(): prediction = lax.psum(partial_pred, ('row', 'col'))  134 us
    psum x1, waiting for transfers between devices, local(): lax.psum((select_rows(batch_index), select_rows(nystrom_index)), ('row',...  112 us
    psum x1, waiting for transfers between devices, local(): correction = lax.psum(product(eigvecs, coeff), 'col')  69.5 us
    dot_general x4, matrix products, product(): jnp.dot(left, right, precision=lax.Precision.HIGHEST, preferred_element_t...  52 us
    dot_general x3, matrix products, kernel(): jnp.dot(left, right.T, precision=lax.Precision.HIGHEST, preferred_element...  38.1 us
    gather x2, local copies, waits for them, and re-layouts, select_rows(): fetched = jnp.take(centres, jnp.clip(local_rows, 0, rows_dev - 1), axis=0)  15.2 us
    psum x1, blocking collectives, local(): coeff = mode_scale[:, None] * lax.psum(mode_terms, 'row')  10.7 us
  transfers between devices with their start and end apart: 4, of which 3 were waited for; matrix products, arithmetic and copies ran while one was open for 11% of the time, Pallas kernels for 0%

commit v1 on v0

v1 whole, which is shorter than its diff:
```python
import functools
import math

import jax
import jax.numpy as jnp
from jax import lax
from jax.experimental import pallas as pl
from jax.experimental.pallas import tpu as pltpu
from jax.sharding import PartitionSpec as P

learning_rate = 0.25
CORES = 2
MESH = pl.DeviceIdType.MESH
VMEM = pl.BlockSpec(memory_space=pltpu.VMEM)
BF16 = jnp.bfloat16
F32 = jnp.float32


def pieces(value, count):
    parts = []
    for step in range(count):
        part = lax.reduce_precision(value, 8, 7)
        parts.append(part.astype(BF16))
        value = value - part
    return parts


def augmented(feats, left):
    rows, width = feats.shape
    unit = math.log2(math.e) / width
    square = pieces(-unit * jnp.sum(feats * feats, axis=1, keepdims=True), 3)
    ones = [jnp.ones((rows, 3), BF16)]
    if left:
        high, low = pieces(feats * (2.0 * unit), 2)
        parts = [high, low, high] + square + ones
    else:
        high, low = pieces(feats, 2)
        parts = [high, high, low] + ones + square
    used = 3 * width + 6
    parts.append(jnp.zeros((rows, -used % 256), BF16))
    return jnp.concatenate(parts, axis=1)


def paired(values):
    return jnp.concatenate(pieces(values, 2), axis=1)


def kmul_body(sub, tile, a_ref, b_ref, w_ref, o_ref):
    rows = a_ref.shape[0]
    wide = w_ref.shape[1]

    def step(index, totals):
        at = pl.ds(pl.multiple_of(index * tile, tile), tile)
        b = b_ref[at, :]
        w = w_ref[at, :]
        result = []
        for part in range(rows // sub):
            a = a_ref[pl.ds(part * sub, sub), :]
            expo = lax.dot_general(
                a, b, (((1,), (1,)), ((), ())), preferred_element_type=F32
            )
            value = jnp.exp2(expo)
            high = value.astype(BF16)
            low = (value - high.astype(F32)).astype(BF16)
            total = totals[part] + jnp.dot(high, w, preferred_element_type=F32)
            result.append(total + jnp.dot(low, w, preferred_element_type=F32))
        return tuple(result)

    zero = tuple(jnp.zeros((sub, wide), F32) for part in range(rows // sub))
    totals = lax.fori_loop(0, b_ref.shape[0] // tile, step, zero)
    for part, total in enumerate(totals):
        o_ref[pl.ds(part * sub, sub), :] = total[:, : wide // 2] + total[:, wide // 2 :]


def kmul(a, b, w, block=512, sub=256, tile=512):
    rows, deep = a.shape
    points, wide = w.shape
    block = min(block, rows)
    return pl.pallas_call(
        functools.partial(kmul_body, min(sub, block), min(tile, points)),
        out_shape=jax.ShapeDtypeStruct((rows, wide // 2), F32),
        grid=(rows // block,),
        in_specs=[
            pl.BlockSpec((block, deep), lambda i: (i, 0)),
            pl.BlockSpec((points, deep), lambda i: (0, 0)),
            pl.BlockSpec((points, wide), lambda i: (0, 0)),
        ],
        out_specs=pl.BlockSpec((block, wide // 2), lambda i: (i, 0)),
    )(a, b, w)


def pick_body(index_ref, cols_ref, o_ref):
    index = index_ref[0]
    rows = cols_ref.shape[1]
    spot = lax.broadcasted_iota(jnp.int32, (rows, index.shape[1]), 0)
    hot = jnp.where(spot == index, 1.0, 0.0).astype(BF16)
    got = jnp.dot(cols_ref[...], hot, preferred_element_type=F32)
    width = cols_ref.shape[0] // 3
    o_ref[0] = (got[:width] + got[width : 2 * width]) + got[2 * width :]


def pick(index, cols, width):
    blocks = index.shape[0]
    return pl.pallas_call(
        pick_body,
        out_shape=jax.ShapeDtypeStruct((blocks, width, 128), F32),
        grid=(blocks,),
        in_specs=[
            pl.BlockSpec((1, 1, 128), lambda i: (i, 0, 0)),
            pl.BlockSpec(cols.shape, lambda i: (0, 0)),
        ],
        out_specs=pl.BlockSpec((1, width, 128), lambda i: (i, 0, 0)),
    )(index, cols)


class Place:
    def __init__(self, xs, cs):
        self.xs, self.cs = xs, cs
        row = lax.axis_index("row")
        self.c = lax.axis_index("col")
        self.k = lax.rem(row, CORES)
        self.x = row // CORES

    def core(self):
        return [(1 - self.k, (self.x * CORES + 1 - self.k, self.c))]

    def line(self):
        spots = [lax.rem(self.x + d, self.xs) for d in range(1, self.xs)]
        return [(s, (s * CORES + self.k, self.c)) for s in spots]

    def cols(self):
        spots = [lax.rem(self.c + d, self.cs) for d in range(1, self.cs)]
        return [(s, (self.x * CORES + self.k, s)) for s in spots]

    def barrier(self):
        sem = pltpu.get_barrier_semaphore()
        everyone = self.core() + self.line() + self.cols()
        for spot, device in everyone:
            pl.semaphore_signal(sem, inc=1, device_id=device, device_id_type=MESH)
        pl.semaphore_wait(sem, len(everyone))


def exchange(partners, source, target, send, recv):
    copies = []
    for d, (spot, device) in enumerate(partners):
        copies.append(
            pltpu.make_async_remote_copy(
                src_ref=source(d, spot),
                dst_ref=target(d, spot),
                send_sem=send.at[d],
                recv_sem=recv.at[d],
                device_id=device,
                device_id_type=MESH,
            )
        )
    for copy in copies:
        copy.start()
    for copy in copies:
        copy.wait()


def summed(first, buffers, count):
    total = first
    for d in range(count):
        total = total + buffers[d]
    return total


def gather(place, o_ref, sems):
    k, x, c = place.k, place.x, place.c
    exchange(place.cols(), lambda d, s: o_ref.at[k, x, c], lambda d, s: o_ref.at[k, x, c], *sems[0])
    exchange(place.line(), lambda d, s: o_ref.at[k, x], lambda d, s: o_ref.at[k, x], *sems[1])
    exchange(place.core(), lambda d, s: o_ref.at[k], lambda d, s: o_ref.at[k], *sems[2])


def reduce_body(xs, cs, in_ref, o_ref, by_core, on_core, by_line, on_line, by_col, *sems):
    place = Place(xs, cs)
    sems = [sems[i : i + 2] for i in range(0, len(sems), 2)]
    place.barrier()
    exchange(place.core(), lambda d, s: in_ref.at[s], lambda d, s: by_core.at[d], *sems[0])
    on_core[...] = in_ref[place.k] + by_core[0]
    exchange(place.line(), lambda d, s: on_core.at[s], lambda d, s: by_line.at[d], *sems[1])
    on_line[...] = summed(on_core[place.x], by_line, xs - 1)
    exchange(place.cols(), lambda d, s: on_line.at[s], lambda d, s: by_col.at[d], *sems[2])
    o_ref[place.k, place.x, place.c] = summed(on_line[place.c], by_col, cs - 1)
    gather(place, o_ref, sems[3:])


def sem_list(counts):
    return [pltpu.SemaphoreType.DMA((n,)) for n in counts for both in range(2)]


def all_reduce(tiles, xs, cs, ident):
    count = tiles.shape[0]
    share = -(-count // (CORES * xs * cs))
    padded = jnp.pad(tiles, ((0, CORES * xs * cs * share - count), (0, 0), (0, 0)))
    piece = (share, 8, 128)
    whole = (CORES, xs, cs) + piece
    out = pl.pallas_call(
        functools.partial(reduce_body, xs, cs),
        out_shape=jax.ShapeDtypeStruct(whole, F32),
        in_specs=[VMEM],
        out_specs=VMEM,
        scratch_shapes=[
            pltpu.VMEM((1, xs, cs) + piece, F32),
            pltpu.VMEM((xs, cs) + piece, F32),
            pltpu.VMEM((xs - 1, cs) + piece, F32),
            pltpu.VMEM((cs,) + piece, F32),
            pltpu.VMEM((cs - 1,) + piece, F32),
        ]
        + sem_list([1, xs - 1, cs - 1, cs - 1, xs - 1, 1]),
        compiler_params=pltpu.CompilerParams(collective_id=ident, has_side_effects=True),
    )(padded.reshape(whole))
    return out.reshape((-1, 8, 128))[:count]


def modes_body(
    xs, cs, part_ref, scale_ref, eig_ref, o_ref,
    by_core, on_core, by_line, terms, by_col, *sems
):
    place = Place(xs, cs)
    sems = [sems[i : i + 2] for i in range(0, len(sems), 2)]
    place.barrier()
    exchange(place.core(), lambda d, s: part_ref, lambda d, s: by_core.at[d], *sems[0])
    on_core[...] = part_ref[...] + by_core[0]
    exchange(place.line(), lambda d, s: on_core, lambda d, s: by_line.at[d], *sems[1])
    coeff = summed(on_core[...], by_line, xs - 1) * scale_ref[...]
    share = eig_ref.shape[0] // cs
    for col in range(cs):
        terms[col] = lax.dot_general(
            coeff,
            eig_ref[pl.ds(col * share, share), :],
            (((1,), (1,)), ((), ())),
            precision=lax.Precision.HIGHEST,
            preferred_element_type=F32,
        )
    exchange(place.cols(), lambda d, s: terms.at[s], lambda d, s: by_col.at[d], *sems[2])
    o_ref[place.k, place.x, place.c] = summed(terms[place.c], by_col, cs - 1)
    gather(place, o_ref, sems[3:])


def corrections(part, scale, eigvecs, xs, cs, ident):
    outs, modes = part.shape
    share = eigvecs.shape[0] // cs
    out = pl.pallas_call(
        functools.partial(modes_body, xs, cs),
        out_shape=jax.ShapeDtypeStruct((CORES, xs, cs, outs, share), F32),
        in_specs=[VMEM] * 3,
        out_specs=VMEM,
        scratch_shapes=[
            pltpu.VMEM((1, outs, modes), F32),
            pltpu.VMEM((outs, modes), F32),
            pltpu.VMEM((xs - 1, outs, modes), F32),
            pltpu.VMEM((cs, outs, share), F32),
            pltpu.VMEM((cs - 1, outs, share), F32),
        ]
        + sem_list([1, xs - 1, cs - 1, cs - 1, xs - 1, 1]),
        compiler_params=pltpu.CompilerParams(collective_id=ident, has_side_effects=True),
    )(part, scale, eigvecs)
    return out.transpose(1, 0, 2, 4, 3).reshape((-1, outs))


def local(xs, cs, centres, weights, targets, batch_index, nystrom_index, eigvecs, mode_scale):
    rows_dev, width = centres.shape
    batch, outs = targets.shape
    block_rows = eigvecs.shape[0]
    offset = lax.axis_index(("row", "col")) * rows_dev

    index = jnp.concatenate([batch_index, nystrom_index]) - offset
    cols = jnp.concatenate(pieces(centres.T, 3), axis=0)
    mine = pick(index.reshape(-1, 1, 128), cols, width)
    feats = all_reduce(mine.reshape(-1, 8, 128), xs, cs, 0)
    feats = feats.reshape(-1, width, 128).transpose(0, 2, 1).reshape(-1, width)

    left = augmented(centres, True)
    right = augmented(feats, False)
    batch_left = augmented(feats[:batch], True)
    nys_block = lax.dynamic_slice_in_dim(
        right, batch + lax.axis_index("row") * block_rows, block_rows, 0
    )

    partial_pred = kmul(right[:batch], left, paired(weights))
    halves = jnp.concatenate([partial_pred[: batch // 2], partial_pred[batch // 2 :]], axis=1)
    summed_pred = all_reduce(halves.reshape(-1, 8, 128), xs, cs, 1).reshape(batch // 2, 2 * outs)
    prediction = jnp.concatenate([summed_pred[:, :outs], summed_pred[:, outs:]], axis=0)
    residual = prediction - targets

    gradient = kmul(nys_block, batch_left, paired(residual))
    part = lax.dot_general(
        gradient,
        eigvecs,
        (((0,), (0,)), ((), ())),
        precision=lax.Precision.HIGHEST,
        preferred_element_type=F32,
    )
    correction = corrections(part, mode_scale[None, :], eigvecs, xs, cs, 2)
    both = learning_rate * jnp.concatenate([residual, -correction], axis=0)
    step = kmul(left, right, paired(both))
    return (residual, step)


def solution(mesh):
    in_specs = (
        P(("row", "col"), None),
        P(("row", "col"), None),
        P(),
        P(),
        P(),
        P("row", "col"),
        P("col"),
    )
    out_specs = (P(), P(("row", "col"), None))
    body = functools.partial(local, mesh.shape["row"] // CORES, mesh.shape["col"])
    return jax.shard_map(body, mesh=mesh, in_specs=in_specs, out_specs=out_specs, check_vma=False)
```

time: 468 us -> 231 us (0.49)
  waiting for transfers between devices: 316 us -> 0 us
  Pallas kernels: 0 us -> 154 us
  matrix products: 95.9 us -> 2.67 us
  local copies, waits for them, and re-layouts: 18.7 us -> 48.2 us
  between operations: 14 us -> 0.9 us
  other arithmetic: 11.7 us -> 23.2 us
  blocking collectives: 10.7 us -> 0 us
    psum x3 -> x0, waiting for transfers between devices: 316 us -> none  [the longest x1 134 us: local(): prediction = lax.psum(partial_pred, ('row', 'col'))]
    pallas_call x0 -> x7, Pallas kernels: none -> 154 us  [the longest x2 64.3 us: all_reduce(): pl.pallas_call(functools.partial(reduce_body, xs, cs), out_shape=jax.Shap...]
    dot_general x9 -> x1, matrix products: 95.9 us -> 2.67 us  [local(): lax.dot_general(gradient, eigvecs, (((0,), (0,)), ((), ())), precision=la...]
    concatenate x0 -> x3, local copies, waits for them, and re-layouts: none -> 17 us  [augmented(): return jnp.concatenate(parts, axis=1)]
    gather x2 -> x0, local copies, waits for them, and re-layouts: 15.2 us -> none  [select_rows(): fetched = jnp.take(centres, jnp.clip(local_rows, 0, rows_dev - 1), axis=0)]
    convert_element_type x0 -> x12, other arithmetic: none -> 13.8 us  [pieces(): parts.append(part.astype(BF16))]
    psum x1 -> x0, blocking collectives: 10.7 us -> none  [local(): coeff = mode_scale[:, None] * lax.psum(mode_terms, 'row')]
    select_n x2 -> x0, other arithmetic: 6.94 us -> none  [select_rows(): return jnp.where(inside[:, None], fetched, 0.0)]
  transfers between devices with their start and end apart: 4 -> 0, of which waited for: 3 -> 0; matrix products, arithmetic and copies ran while one was open for 11% -> 0% of each run, Pallas kernels for 0% -> 0%
where the time goes in v1:
time: 231 us; the launch traced here: 229 us
  Pallas kernels  154 us (67%)
  local copies, waits for them, and re-layouts  48.2 us (21%)
  other arithmetic  23.2 us (10%)
  matrix products  2.67 us (1%)
    pallas_call x2, Pallas kernels, all_reduce(): pl.pallas_call(functools.partial(reduce_body, xs, cs), out_shape=jax.Shap...  64.3 us
    pallas_call x3, Pallas kernels, kmul(): pl.pallas_call(functools.partial(kmul_body, min(sub, block), min(tile, po...  40.2 us
    pallas_call x1, Pallas kernels, corrections(): pl.pallas_call(functools.partial(modes_body, xs, cs), out_shape=jax.Shape...  28.3 us
    pallas_call x1, Pallas kernels, pick(): pl.pallas_call(pick_body, out_shape=jax.ShapeDtypeStruct((blocks, width,...  21 us
    concatenate x3, local copies, waits for them, and re-layouts, augmented(): return jnp.concatenate(parts, axis=1)  17 us
    convert_element_type x12, other arithmetic, pieces(): parts.append(part.astype(BF16))  13.8 us
    unnamed x17, local copies, waits for them, and re-layouts  6.95 us
    reduce_precision x4, local copies, waits for them, and re-layouts, pieces(): part = lax.reduce_precision(value, 8, 7)  4.98 us

profile of v1, /device:TPU:0, one launch (start us, length us, event | category | flops | bytes accessed | tf_op | source)
XLA Modules:
  0.0 228.7 jit_solution(2197653277658365516)
XLA Ops:
  3.4 21.0 %shard_map.86 = f32[36,64,128]{2,1,0:T(8,128)} custom-call(s32[36,1,128]{2,1,0:T(1,128)} %sub.123.index_ref, bf16[192,2048]{1,0:T(8,128)(2,1)} %pad_maximum_fusion.1.cols_ref), custom_call_target="tpu_custom_call" | custom-call | tf_op jit(solution)/shard_map/pallas_call | solution.py:104
  24.4 40.4 %shard_map.87 = f32[2,2,8,9,8,128]{5,4,3,2,1,0:T(8,128)} custom-call(f32[2,2,8,9,8,128]{5,4,3,2,1,0:T(8,128)} %bitcast.38), custom_call_target="tpu_custom_call" | custom-call | tf_op jit(solution)/shard_map/pallas_call | solution.py:199
  64.8 1.8 copy.31
  67.3 2.1 copy.32
  69.5 2.1 copy.33
  71.6 4.2 %fusion.3 = (bf16[4608,1]{1,0:T(8,128)(2,1)}, bf16[4608,1]{1,0:T(8,128)(2,1)}) fusion(f32[4608,1]{1,0:T(8,128)} %copy.32, f32[4608,1]{1,0:T(8,128)} %copy.33), kind=kLoop, calls=%fused_computation.9 | loop fusion | flops 27648 | bytes 55296 | tf_op jit(solution)/shard_map/convert_element_type | solution.py:23
  75.9 1.5 copy.34
  77.4 1.4 fusion.1
  81.2 9.9 %concatenate.35.b_ref = bf16[4608,256]{1,0:T(8,128)(2,1)} concatenate(bf16[4608,64]{1,0:T(8,128)(2,1)S(1)} %get-tuple-element.19, bf16[4608,64]{1,0:T(8,128)(2,1)S(1)} %get-tuple-element.19, bf16[4608,64]{1,0:T(8,128)(2,1)} %get-tuple-element.18, bf16[4608,3]{1,0:T(8,128)(2,1)} %broadcast_in_dim.24, bf16[4608,1]{1,0:T(8,128)(2,1)} %copy.34, bf16[4608,1]{1,0:T(8,128)(2,1)} %get-tuple-element.13, ...), dimensions={1} | concatenate | bytes 4718592 | tf_op jit(solution)/shard_map/concatenate | solution.py:41
  91.1 1.7 slice.25.a_ref
  96.6 2.8 %fusion.9 = (bf16[2048,1]{1,0:T(8,128)(2,1)}, bf16[2048,1]{1,0:T(8,128)(2,1)}) fusion(f32[2048,1]{1,0:T(8,128)} %copy.37, f32[2048,1]{1,0:T(8,128)} %copy.38), kind=kLoop, calls=%fused_computation.22 | loop fusion | flops 12288 | bytes 24576 | tf_op jit(solution)/shard_map/convert_element_type | solution.py:23
  101.8 2.2 fusion.7
  105.7 5.9 %concatenate.36.b_ref.a_ref = bf16[2048,256]{1,0:T(8,128)(2,1)} concatenate(bf16[2048,64]{1,0:T(8,128)(2,1)S(1)} %get-tuple-element.25, bf16[2048,64]{1,0:T(8,128)(2,1)} %get-tuple-element.24, bf16[2048,64]{1,0:T(8,128)(2,1)S(1)} %get-tuple-element.25, bf16[2048,1]{1,0:T(8,128)(2,1)} %copy.39, bf16[2048,1]{1,0:T(8,128)(2,1)} %get-tuple-element.21, ...), dimensions={1} | concatenate | bytes 2097152 | tf_op jit(solution)/shard_map/concatenate | solution.py:41
  112.5 1.4 copy.40
  113.9 2.4 %copy.41 = f32[2048,64]{1,0:T(8,128)} copy(f32[2048,64]{0,1:T(8,128)} %param.8) | data formatting | bytes 1048576 | tf_op args[1]
  118.7 5.4 %shard_map.88 = f32[512,64]{1,0:T(8,128)} custom-call(bf16[512,256]{1,0:T(8,128)(2,1)} %slice.25.a_ref, bf16[2048,256]{1,0:T(8,128)(2,1)} %concatenate.36.b_ref.a_ref, bf16[2048,128]{1,0:T(8,128)(2,1)} %pad_maximum_fusion.2.w_ref), custom_call_target="tpu_custom_call" | custom-call | tf_op jit(solution)/shard_map/pallas_call | solution.py:79
  125.9 24.0 %shard_map.89 = f32[2,2,8,1,8,128]{5,4,3,2,1,0:T(8,128)} custom-call(f32[2,2,8,1,8,128]{5,4,3,2,1,0:T(8,128)} %bitcast.40), custom_call_target="tpu_custom_call" | custom-call | tf_op jit(solution)/shard_map/pallas_call | solution.py:199
  151.9 1.9 constant_dynamic-slice_fusion.a_ref
  155.8 3.5 %shard_map.90 = f32[1024,64]{1,0:T(8,128)} custom-call(bf16[1024,256]{1,0:T(8,128)(2,1)} %constant_dynamic-slice_fusion.a_ref, bf16[512,256]{1,0:T(8,128)(2,1)} %concatenate.40.b_ref, bf16[512,128]{1,0:T(8,128)(2,1)} %pad_maximum_fusion.4.w_ref), custom_call_target="tpu_custom_call" | custom-call | tf_op jit(solution)/shard_map/pallas_call | solution.py:79
  159.3 2.7 %fusion.24.part_ref = f32[64,128]{1,0:T(8,128)} fusion(f32[1024,64]{1,0:T(8,128)} %shard_map.90, f32[1024,128]{1,0:T(8,128)S(1)} %copy-done.2), kind=kOutput, calls=%fused_computation.66 | convolution fusion | flops 100663296 | bytes 819200 | tf_op jit(solution)/shard_map/dot_general | solution.py:289
  161.9 28.3 %shard_map.91 = f32[2,2,8,64,128]{4,3,2,1,0:T(8,128)} custom-call(f32[64,128]{1,0:T(8,128)} %fusion.24.part_ref, f32[1,128]{1,0:T(1,128)} %bitcast.45, f32[1024,128]{1,0:T(8,128)} %eig_ref.1), custom_call_target="tpu_custom_call" | custom-call | tf_op jit(solution)/shard_map/pallas_call | solution.py:245
  192.6 1.7 pad_maximum_fusion.w_ref
  194.3 31.3 %shard_map.92 = f32[2048,64]{1,0:T(8,128)} custom-call(bf16[2048,256]{1,0:T(8,128)(2,1)} %concatenate.36.b_ref.a_ref, bf16[4608,256]{1,0:T(8,128)(2,1)} %concatenate.35.b_ref, bf16[4608,128]{1,0:T(8,128)(2,1)} %pad_maximum_fusion.w_ref), custom_call_target="tpu_custom_call" | custom-call | tf_op jit(solution)/shard_map/pallas_call | solution.py:79
  225.6 2.3 %copy.49 = f32[2048,64]{0,1:T(8,128)} copy(f32[2048,64]{1,0:T(8,128)} %shard_map.92) | data formatting | bytes 1048576
  (56 shorter events, 26.0 us)
Async XLA Ops:
  0.6 2.2 copy-start.5
  0.6 2.2 copy-start.4
  96.6 3.9 %copy-start = (f32[2048,64]{0,1:T(8,128)S(1)}, f32[2048,64]{0,1:T(8,128)}, u32[]{:S(2)}) copy-start(f32[2048,64]{0,1:T(8,128)} %param.7) | copy-start | bytes 1572868
  105.7 5.9 %copy-start.1 = (f32[2048,64]{0,1:T(8,128)S(1)}, f32[2048,64]{0,1:T(8,128)}, u32[]{:S(2)}) copy-start(f32[2048,64]{0,1:T(8,128)} %param.8) | copy-start | bytes 1572868
  118.7 32.2 %copy-start.3 = (f32[512,64]{0,1:T(8,128)S(1)}, f32[512,64]{0,1:T(8,128)}, u32[]{:S(2)}) copy-start(f32[512,64]{0,1:T(8,128)} %param.9) | copy-start | bytes 393220
  154.3 5.0 %copy-start.2 = (f32[1024,128]{1,0:T(8,128)S(1)}, f32[1024,128]{1,0:T(8,128)}, u32[]{:S(2)}) copy-start(f32[1024,128]{1,0:T(8,128)} %eig_ref.1) | copy-start | bytes 1572868

commit v2 on v0

v2 whole, which is shorter than its diff:
```python
import functools
import math

import jax
import jax.numpy as jnp
from jax import lax
from jax.experimental import pallas as pl
from jax.experimental.pallas import tpu as pltpu
from jax.sharding import PartitionSpec as P

learning_rate = 0.25
CORES = 2
MESH = pl.DeviceIdType.MESH
VMEM = pl.BlockSpec(memory_space=pltpu.VMEM)
BF16 = jnp.bfloat16
F32 = jnp.float32


def pieces(value, count):
    parts = []
    for step in range(count):
        part = value.astype(BF16).astype(F32)
        parts.append(part)
        value = value - part
    return parts


def paired(value):
    return jnp.concatenate(pieces(value, 2), axis=0).astype(BF16)


def augmented(feats, left):
    width, count = feats.shape
    unit = math.log2(math.e) / width
    square = pieces(-unit * jnp.sum(feats * feats, axis=0, keepdims=True), 3)
    if left:
        high, low = pieces(feats * (2.0 * unit), 2)
        parts, first, one = [high, low, high], 0, 3
    else:
        high, low = pieces(feats, 2)
        parts, first, one = [high, high, low], 3, 0
    spot = lax.broadcasted_iota(jnp.int32, (8, count), 0)
    tail = jnp.where((spot >= one) & (spot < one + 3), 1.0, 0.0)
    for at, part in enumerate(square):
        tail = jnp.where(spot == first + at, part, tail)
    deep = depth_of(width)
    fill = jnp.zeros((deep - 3 * width - 8, count), F32)
    return jnp.concatenate(parts + [tail, fill], axis=0)


def depth_of(width):
    return -(-(3 * width + 8) // 128) * 128


def largest(count, limit):
    return max(d for d in range(1, limit + 1) if count % d == 0)


def kmul(a_ref, b_ref, w_ref, o_ref, finish):
    points, outs = a_ref.shape[0], o_ref.shape[0]
    wide = b_ref.shape[1]
    sub = min(512, points)
    parts = largest(points // sub, 3)
    tile = min(512, wide)

    def across(i, unused):
        to = pl.ds(pl.multiple_of(i * tile, tile), tile)
        b = b_ref[:, to]

        def down(j, total):
            for part in range(parts):
                at = pl.ds(pl.multiple_of((j * parts + part) * sub, sub), sub)
                value = jnp.exp2(jnp.dot(a_ref[at, :], b, preferred_element_type=F32))
                high = value.astype(BF16)
                low = (value - high.astype(F32)).astype(BF16)
                w = w_ref[:, at]
                total = total + (
                    jnp.dot(w, high, preferred_element_type=F32)
                    + jnp.dot(w, low, preferred_element_type=F32)
                )
            return total

        total = lax.fori_loop(0, points // (sub * parts), down, jnp.zeros((2 * outs, tile), F32))
        o_ref[:, to] = finish(total[:outs] + total[outs:], to)
        return unused

    lax.fori_loop(0, wide // tile, across, 0)


class Place:
    def __init__(self, xs, cs):
        self.xs, self.cs = xs, cs
        row = lax.axis_index("row")
        self.c = lax.axis_index("col")
        self.k = lax.rem(row, CORES)
        self.x = row // CORES

    def core(self):
        return [(1 - self.k, (self.x * CORES + 1 - self.k, self.c))]

    def line(self):
        spots = [lax.rem(self.x + d, self.xs) for d in range(1, self.xs)]
        return [(s, (s * CORES + self.k, self.c)) for s in spots]

    def cols(self):
        spots = [lax.rem(self.c + d, self.cs) for d in range(1, self.cs)]
        return [(s, (self.x * CORES + self.k, s)) for s in spots]

    def barrier(self):
        sem = pltpu.get_barrier_semaphore()
        everyone = self.core() + self.line() + self.cols()
        for spot, device in everyone:
            pl.semaphore_signal(sem, inc=1, device_id=device, device_id_type=MESH)
        pl.semaphore_wait(sem, len(everyone))


def start(partners, source, target, sems):
    copies = []
    for d, (spot, device) in enumerate(partners):
        copies.append(
            pltpu.make_async_remote_copy(
                src_ref=source(d, spot),
                dst_ref=target(d, spot),
                send_sem=sems[0].at[d],
                recv_sem=sems[1].at[d],
                device_id=device,
                device_id_type=MESH,
            )
        )
    for copy in copies:
        copy.start()
    return copies


def finish(copies):
    for copy in copies:
        copy.wait()


def summed(first, buffers, count):
    total = first
    for d in range(count):
        total = total + buffers[d]
    return total


def gather_steps(place, o_ref, sems):
    k, x, c = place.k, place.x, place.c
    copies = start(place.cols(), lambda d, s: o_ref.at[k, x, c], lambda d, s: o_ref.at[k, x, c], sems[0])
    yield
    finish(copies)
    copies = start(place.line(), lambda d, s: o_ref.at[k, x], lambda d, s: o_ref.at[k, x], sems[1])
    yield
    finish(copies)
    copies = start(place.core(), lambda d, s: o_ref.at[k], lambda d, s: o_ref.at[k], sems[2])
    yield
    finish(copies)


def reduce_steps(place, bufs, sems):
    in_ref, by_core, on_core, by_line, on_line, by_col, o_ref = bufs
    copies = start(place.core(), lambda d, s: in_ref.at[s], lambda d, s: by_core.at[d], sems[0])
    yield
    finish(copies)
    on_core[...] = in_ref[place.k] + by_core[0]
    copies = start(place.line(), lambda d, s: on_core.at[s], lambda d, s: by_line.at[d], sems[1])
    yield
    finish(copies)
    on_line[...] = summed(on_core[place.x], by_line, place.xs - 1)
    copies = start(place.cols(), lambda d, s: on_line.at[s], lambda d, s: by_col.at[d], sems[2])
    yield
    finish(copies)
    o_ref[place.k, place.x, place.c] = summed(on_line[place.c], by_col, place.cs - 1)
    yield from gather_steps(place, o_ref, sems[3:])


def mode_steps(place, bufs, sems, scale_ref, eig_ref):
    part, by_core, on_core, by_line, terms, by_col, o_ref = bufs
    copies = start(place.core(), lambda d, s: part, lambda d, s: by_core.at[d], sems[0])
    yield
    finish(copies)
    on_core[...] = part[...] + by_core[0]
    copies = start(place.line(), lambda d, s: on_core, lambda d, s: by_line.at[d], sems[1])
    yield
    finish(copies)
    coeff = summed(on_core[...], by_line, place.xs - 1) * scale_ref[...]
    correction = lax.dot_general(
        coeff,
        eig_ref[...],
        (((1,), (1,)), ((), ())),
        precision=lax.Precision.HIGHEST,
        preferred_element_type=F32,
    )
    store_tiles(correction, 0, lambda t, tile: place_in(terms, t, tile))
    copies = start(place.cols(), lambda d, s: terms.at[s], lambda d, s: by_col.at[d], sems[2])
    yield
    finish(copies)
    o_ref[place.k, place.x, place.c] = summed(terms[place.c], by_col, place.cs - 1)
    yield from gather_steps(place, o_ref, sems[3:])


def spot_of(shape, t):
    row, rest = divmod(t, shape[2] * shape[3])
    return (row % CORES, row // CORES) + divmod(rest, shape[3])


def place_in(terms, t, tile):
    terms[divmod(t, terms.shape[1])] = tile


def store_tiles(value, block, put):
    high = value.shape[0] // 8
    for j in range(value.shape[1] // 128):
        for g in range(high):
            put((block + j) * high + g, value[8 * g : 8 * g + 8, 128 * j : 128 * j + 128])


def store_all(buf, block, value):
    def put(t, tile):
        buf[spot_of(buf.shape, t)] = tile

    store_tiles(value, block, put)


def load_tiles(get, high, block, blocks):
    columns = []
    for j in range(block, block + blocks):
        columns.append(jnp.concatenate([get(j * high + g) for g in range(high)], axis=0))
    return jnp.concatenate(columns, axis=1) if blocks > 1 else columns[0]


def load_all(buf, high, block, blocks):
    return load_tiles(lambda t: buf[spot_of(buf.shape, t)], high, block, blocks)


def reduce_shapes(tiles, xs, cs):
    share = -(-tiles // (CORES * xs * cs))
    piece = (share, 8, 128)
    shapes = [
        (CORES, xs, cs) + piece,
        (1, xs, cs) + piece,
        (xs, cs) + piece,
        (xs - 1, cs) + piece,
        (cs,) + piece,
        (cs - 1,) + piece,
        (CORES, xs, cs) + piece,
    ]
    return [pltpu.VMEM(shape, F32) for shape in shapes]


CHUNK = 512


def main_body(
    xs, cs, batch, points, centres, weights, targets, index, scale, eig,
    residual, both, right, left, *scratch
):
    width, rows = centres.shape
    outs = targets.shape[0]
    high = width // 8
    b_bufs, n_bufs, p_bufs, m_bufs = (scratch[i : i + 7] for i in range(0, 28, 7))
    split, left_rows, batch_right, batch_left, block_right, pairs, pred, grad = scratch[28:36]
    sems = [scratch[i : i + 2] for i in range(36, len(scratch), 2)]
    place = Place(xs, cs)
    place.barrier()

    def pick(at, count):
        spot = lax.broadcasted_iota(jnp.int32, (rows, count), 0)
        hot = jnp.where(spot == index[:, at : at + count], 1.0, 0.0).astype(BF16)
        got = jnp.dot(split[...], hot, preferred_element_type=F32)
        return (got[:width] + got[width : 2 * width]) + got[2 * width :]

    def pick_points(first, last):
        for at in range(first, last, CHUNK):
            count = min(CHUNK, last - at)
            store_all(n_bufs[0], at // 128, pick(batch + at, count))

    def share(step, steps):
        size = -(-points // (steps * 128)) * 128
        return min(step * size, points), min(step * size + size, points)

    split[...] = jnp.concatenate(pieces(centres[...], 3), axis=0).astype(BF16)
    for bufs in (b_bufs, n_bufs, p_bufs, m_bufs):
        if bufs is not m_bufs:
            bufs[0][...] = jnp.zeros_like(bufs[0])
    for at in range(0, batch, CHUNK):
        store_all(b_bufs[0], at // 128, pick(at, min(CHUNK, batch - at)))
    of_batch = reduce_steps(place, b_bufs, sems[:6])
    of_points = reduce_steps(place, n_bufs, sems[6:12])
    next(of_batch)
    pick_points(*share(0, 4))
    next(of_batch)
    pick_points(*share(1, 4))
    next(of_batch)
    pick_points(*share(2, 4))
    pick_points(*share(3, 4))
    next(of_points)
    next(of_batch)
    for at in range(0, rows, CHUNK):
        to = slice(at, min(at + CHUNK, rows))
        form = augmented(centres[:, to], True)
        left[:, to] = form.astype(BF16)
        left_rows[to, :] = form.T.astype(BF16)
    pairs[...] = paired(weights[...])
    next(of_batch)
    next(of_points)
    next(of_batch)
    next(of_batch, None)

    feats = load_all(b_bufs[6], high, 0, batch // 128)
    form = augmented(feats, False)
    batch_right[...] = form.astype(BF16)
    kmul(left_rows, batch_right, pairs, pred, lambda total, to: total)
    store_all(p_bufs[0], 0, pred[...])
    of_pred = reduce_steps(place, p_bufs, sems[12:18])
    next(of_pred)
    right[:batch, :] = form.T.astype(BF16)
    batch_left[...] = augmented(feats, True).T.astype(BF16)
    next(of_pred)
    next(of_points)
    next(of_pred)
    next(of_pred)
    next(of_points)
    next(of_pred)
    next(of_pred)
    next(of_pred, None)

    rest = load_all(p_bufs[6], outs // 8, 0, batch // 128) - targets[...]
    residual[...] = rest
    both[:, :batch] = paired(learning_rate * rest)
    pairs_rest = paired(rest)
    next(of_points)
    mine = n_bufs[6].at[place.k, place.x]
    block = eig.shape[0]
    feats = load_tiles(lambda t: mine[divmod(t, mine.shape[1])], high, 0, block // 128)
    block_right[...] = augmented(feats, False).astype(BF16)
    pairs[:, :batch] = pairs_rest
    kmul(batch_left, block_right, pairs.at[:, :batch], grad, lambda total, to: total)
    m_bufs[0][...] = jnp.dot(
        grad[...], eig[...], precision=lax.Precision.HIGHEST, preferred_element_type=F32
    )
    of_modes = mode_steps(place, m_bufs, sems[18:24], scale, eig)

    def point_forms(first, last):
        for at in range(first, last, CHUNK):
            count = min(CHUNK, last - at)
            feats = load_all(n_bufs[6], high, at // 128, count // 128)
            right[batch + at : batch + at + count, :] = augmented(feats, False).T.astype(BF16)

    next(of_modes)
    next(of_modes)
    next(of_points)
    next(of_modes)
    next(of_points, None)
    point_forms(*share(0, 3))
    next(of_modes)
    point_forms(*share(1, 3))
    next(of_modes)
    point_forms(*share(2, 3))
    next(of_modes)
    next(of_modes, None)
    for at in range(0, points, CHUNK):
        count = min(CHUNK, points - at)
        correction = load_all(m_bufs[6], outs // 8, at // 128, count // 128)
        both[:, batch + at : batch + at + count] = paired(-learning_rate * correction)


def step_body(right, left, both, o_ref):
    kmul(right, left, both, o_ref, lambda total, to: total)


def local(xs, cs, centres, weights, targets, batch_index, nystrom_index, eigvecs, mode_scale):
    rows, width = centres.shape
    batch, outs = targets.shape
    points = nystrom_index.shape[0]
    block, modes = eigvecs.shape
    deep = depth_of(width)
    total = batch + points
    offset = lax.axis_index(("row", "col")) * rows
    index = jnp.concatenate([batch_index, nystrom_index])[None, :] - offset
    mode_share = -(-(outs // 8 * block // 128) // cs)
    piece = (mode_share, 8, 128)
    sums = [1, xs - 1, cs - 1, cs - 1, xs - 1, 1] * 4
    residual, both, right, left = pl.pallas_call(
        functools.partial(main_body, xs, cs, batch, points),
        out_shape=[
            jax.ShapeDtypeStruct((outs, batch), F32),
            jax.ShapeDtypeStruct((2 * outs, total), BF16),
            jax.ShapeDtypeStruct((total, deep), BF16),
            jax.ShapeDtypeStruct((deep, rows), BF16),
        ],
        in_specs=[VMEM] * 6,
        out_specs=[VMEM] * 4,
        scratch_shapes=reduce_shapes(width // 8 * batch // 128, xs, cs)
        + reduce_shapes(width // 8 * points // 128, xs, cs)
        + reduce_shapes(outs // 8 * batch // 128, xs, cs)
        + [
            pltpu.VMEM((outs, modes), F32),
            pltpu.VMEM((1, outs, modes), F32),
            pltpu.VMEM((outs, modes), F32),
            pltpu.VMEM((xs - 1, outs, modes), F32),
            pltpu.VMEM((cs,) + piece, F32),
            pltpu.VMEM((cs - 1,) + piece, F32),
            pltpu.VMEM((CORES, xs, cs) + piece, F32),
            pltpu.VMEM((3 * width, rows), BF16),
            pltpu.VMEM((rows, deep), BF16),
            pltpu.VMEM((deep, batch), BF16),
            pltpu.VMEM((batch, deep), BF16),
            pltpu.VMEM((deep, block), BF16),
            pltpu.VMEM((2 * outs, rows), BF16),
            pltpu.VMEM((outs, batch), F32),
            pltpu.VMEM((outs, block), F32),
        ]
        + [pltpu.SemaphoreType.DMA((n,)) for n in sums for both_ways in range(2)],
        compiler_params=pltpu.CompilerParams(collective_id=0, has_side_effects=True),
    )(centres.T, weights.T, targets.T, index, mode_scale[None, :], eigvecs)
    step = pl.pallas_call(
        step_body,
        out_shape=jax.ShapeDtypeStruct((outs, rows), F32),
        in_specs=[VMEM] * 3,
        out_specs=VMEM,
    )(right, left, both)
    return (residual.T, step.T)


def solution(mesh):
    in_specs = (
        P(("row", "col"), None),
        P(("row", "col"), None),
        P(),
        P(),
        P(),
        P("row", "col"),
        P("col"),
    )
    out_specs = (P(), P(("row", "col"), None))
    body = functools.partial(local, mesh.shape["row"] // CORES, mesh.shape["col"])
    return jax.shard_map(body, mesh=mesh, in_specs=in_specs, out_specs=out_specs, check_vma=False)
```

time: 468 us -> 104 us (0.22)
  waiting for transfers between devices: 316 us -> 0 us
  Pallas kernels: 0 us -> 101 us
  matrix products: 95.9 us -> 0 us
  local copies, waits for them, and re-layouts: 18.7 us -> 0.66 us
  between operations: 14 us -> 0.65 us
  blocking collectives: 10.7 us -> 0 us
  other arithmetic: 11.7 us -> 1.34 us
    psum x3 -> x0, waiting for transfers between devices: 316 us -> none  [the longest x1 134 us: local(): prediction = lax.psum(partial_pred, ('row', 'col'))]
    pallas_call x0 -> x2, Pallas kernels: none -> 101 us  [the longest x1 80.7 us: local(): pl.pallas_call(functools.partial(main_body, xs, cs, batch, points), out_s...]
    dot_general x9 -> x0, matrix products: 95.9 us -> none  [the longest x4 52 us: product(): jnp.dot(left, right, precision=lax.Precision.HIGHEST, preferred_element_t...]
    gather x2 -> x0, local copies, waits for them, and re-layouts: 15.2 us -> none  [select_rows(): fetched = jnp.take(centres, jnp.clip(local_rows, 0, rows_dev - 1), axis=0)]
    psum x1 -> x0, blocking collectives: 10.7 us -> none  [local(): coeff = mode_scale[:, None] * lax.psum(mode_terms, 'row')]
    select_n x2 -> x0, other arithmetic: 6.94 us -> none  [select_rows(): return jnp.where(inside[:, None], fetched, 0.0)]
  transfers between devices with their start and end apart: 4 -> 0, of which waited for: 3 -> 0; matrix products, arithmetic and copies ran while one was open for 11% -> 0% of each run, Pallas kernels for 0% -> 0%
where the time goes in v2:
time: 104 us
  Pallas kernels  101 us (97%)
  other arithmetic  1.34 us (1%)
    pallas_call x1, Pallas kernels, local(): pl.pallas_call(functools.partial(main_body, xs, cs, batch, points), out_s...  80.7 us
    pallas_call x1, Pallas kernels, local(): pl.pallas_call(step_body, out_shape=jax.ShapeDtypeStruct((outs, rows), F3...  20.3 us

profile of v2, /device:TPU:0, one launch (start us, length us, event | category | flops | bytes accessed | tf_op | source)
XLA Modules:
  0.0 103.7 jit_solution(10109961377852213103)
XLA Ops:
  0.6 1.3 %add_subtract_fusion.index = s32[1,4608]{1,0:T(1,128)} fusion(s32[1,4096]{1,0:T(1,128)} %bitcast.13, s32[1,512]{1,0:T(1,128)} %bitcast.14, s32[]{:T(128)S(6)} %mul.7), kind=kLoop, calls=%fused_computation | loop fusion | flops 9216 | bytes 36868 | tf_op jit(solution)/shard_map/sub | solution.py:380
  2.0 80.7 %shard_map.86 = (f32[64,512]{1,0:T(8,128)}, bf16[128,4608]{1,0:T(8,128)(2,1)}, bf16[4608,256]{1,0:T(8,128)(2,1)}, bf16[256,2048]{1,0:T(8,128)(2,1)}) custom-call(f32[64,2048]{1,0:T(8,128)} %bitcast.8, f32[64,2048]{1,0:T(8,128)} %bitcast.9, f32[64,512]{1,0:T(8,128)} %bitcast.11, s32[1,4608]{1,0:T(1,128)} %add_subtract_fusion.index, f32[1,128]{1,0:T(1,128)} %bitcast.15, ...), custom_call_target="tpu_custom_call" | custom-call | tf_op jit(solution)/shard_map/pallas_call | solution.py:384
  82.6 0.0 copy-start
  82.7 20.3 %shard_map.87 = f32[64,2048]{1,0:T(8,128)} custom-call(bf16[4608,256]{1,0:T(8,128)(2,1)} %get-tuple-element.7.right, bf16[256,2048]{1,0:T(8,128)(2,1)} %get-tuple-element.8.left, bf16[128,4608]{1,0:T(8,128)(2,1)} %get-tuple-element.9.both), custom_call_target="tpu_custom_call" | custom-call | tf_op jit(solution)/shard_map/pallas_call | solution.py:417
  103.0 0.0 copy-done
  103.0 0.7 copy.10
Async XLA Ops:
  82.6 20.3 %copy-start = (f32[64,512]{1,0:T(8,128)S(1)}, f32[64,512]{1,0:T(8,128)}, u32[]{:S(2)}) copy-start(f32[64,512]{1,0:T(8,128)} %get-tuple-element.6) | copy-start | bytes 393220
